TPU v7x, 256 devices: a whole 4x4x8 slice. The times are simulated.
256 devices in a mesh: gx: 32 (over z_hi, x, core), gy: 8 (over z_lo, y).
Axes of the slice: x: 4, y: 4, z: 8 (z_hi: 4, z_lo: 2; z = z_hi * 2 + z_lo), core: 2. Of those that a mesh axis runs over, the one named last changes fastest.
Arguments:
- checkpoint: float32 [19, 256, 2048], P(None, 'gx', 'gy'), as said below
- cotangent: float32 [19, 256, 2048], P(None, 'gx', 'gy'), may hold values from -6 to 6
- blade_area: float32 [1536], replicated, may hold values from 0.5 to 2
- hub_tile: int32 [16], replicated, may hold values from 0 to 255
- point_side: int32 [1536], replicated, may hold values from 0 to 8
- point_local: int32 [1536], replicated, may hold values from 0 to 2047
Outputs:
- grad_checkpoint: float32 [19, 256, 2048], P(None, 'gx', 'gy')
- grad_area: float32 [1536], replicated
Inputs may be any that keep to these rules, and one draw needn't show every extreme that they name: `hub_tile`: tile ids count every tile of the slab. `point_side`: every actuator point lies in its hub tile or one of the eight tiles around it. `checkpoint`: populations are positive and near a local equilibrium with density near one and streamwise velocity near 0.08.
All inputs are finite; a program needn't handle non-finite values.
Results may differ from a plain program's by a relative error of at most 0.0003.
Values sent between devices are 32-bit elements; how exact they have to be, the bound alone decides.
No kernel may reach another device: no remote copies, remote signals or barrier semaphores. Data moves between devices by JAX's collectives and lax.ppermute only.
A program may use at most 128 MiB of HBM per device.

v0:
```python
import jax
import jax.numpy as jnp
import numpy as np
from jax import lax
from jax.sharding import PartitionSpec as P

NZ = 16
STEPS = 4
NTURB = 16
PTS = 96
TAU_ZERO = 0.52
SMAGORINSKY = 0.17 * 0.17
TINY = 1e-10
THRUST = 4.0
GHOST_RATES = np.array([1.05, 1.15, 1.25, 1.35, 1.45, 1.55, 1.65, 1.75, 1.85])


def extended(value, sides, width):
    for axis, dim in sides:
        size, length = (lax.axis_size(axis), value.shape[dim])
        up = [(i, (i + 1) % size) for i in range(size)]
        down = [(j, i) for i, j in up]
        last = lax.slice_in_dim(value, length - width, length, axis=dim)
        first = lax.slice_in_dim(value, 0, width, axis=dim)
        before = lax.ppermute(last, axis, up)
        after = lax.ppermute(first, axis, down)
        value = jnp.concatenate([before, value, after], axis=dim)
    return value


def lattice():
    axis_part = [(1, 0, 0), (-1, 0, 0), (0, 1, 0), (0, -1, 0), (0, 0, 1), (0, 0, -1)]
    edge_part = [
        (1, 1, 0),
        (-1, -1, 0),
        (1, -1, 0),
        (-1, 1, 0),
        (1, 0, 1),
        (-1, 0, -1),
        (1, 0, -1),
        (-1, 0, 1),
        (0, 1, 1),
        (0, -1, -1),
        (0, 1, -1),
        (0, -1, 1),
    ]
    vectors = np.array([(0, 0, 0)] + axis_part + edge_part) * 1.0
    weights = np.array([1.0 / 3.0] + [1.0 / 18.0] * 6 + [1.0 / 36.0] * 12)
    opposite = np.array(
        [int(np.argmin(np.abs(vectors + vectors[column]).sum(1))) for column in range(19)]
    )
    return (vectors, weights, opposite)


def orthonormal(monomials, weights):
    rows = []
    for entry in monomials:
        vector = entry * 1.0
        for sweep in range(2):
            for other in rows:
                vector = vector - np.sum(weights * vector * other) * other
        vector = vector / np.sqrt(np.sum(weights * vector * vector))
        rows.append(vector)
    return np.stack(rows, 0)


def tables():
    vectors, weights, opposite = lattice()
    along_x, along_y, along_z = (vectors[:, 0], vectors[:, 1], vectors[:, 2])
    monomials = [
        np.ones(19),
        along_x,
        along_y,
        along_z,
        along_x * along_x,
        along_y * along_y,
        along_z * along_z,
        along_x * along_y,
        along_x * along_z,
        along_y * along_z,
        along_x * along_y * along_y,
        along_x * along_z * along_z,
        along_y * along_x * along_x,
        along_y * along_z * along_z,
        along_z * along_x * along_x,
        along_z * along_y * along_y,
        along_x * along_x * along_y * along_y,
        along_x * along_x * along_z * along_z,
        along_y * along_y * along_z * along_z,
    ]
    basis = orthonormal(monomials, weights)
    second = weights[:, None] * basis[4:10].T
    ghost = weights[:, None] * basis[10:].T * GHOST_RATES[None, :]
    stress = np.stack(
        [
            along_x * along_x,
            along_y * along_y,
            along_z * along_z,
            along_x * along_y,
            along_x * along_z,
            along_y * along_z,
        ],
        0,
    )
    push = 3.0 * weights * along_x
    return {
        "vectors": vectors,
        "weights": weights,
        "opposite": opposite,
        "high": jnp.asarray(basis[4:], jnp.float32),
        "second": jnp.asarray(second, jnp.float32),
        "ghost": jnp.asarray(ghost, jnp.float32),
        "stress": jnp.asarray(stress, jnp.float32),
        "push": jnp.asarray(push, jnp.float32),
        "velt": jnp.asarray(vectors.T, jnp.float32),
        "wvec": jnp.asarray(weights, jnp.float32),
        "vecs": jnp.asarray(vectors, jnp.float32),
    }


def streamwise_velocity(flat, table):
    density = jnp.sum(flat, 0)
    momentum = jnp.dot(table["velt"], flat, precision=lax.Precision.HIGHEST)
    return momentum[0] / density


def collide(flat, force, table):
    density = jnp.sum(flat, 0)
    momentum = jnp.dot(table["velt"], flat, precision=lax.Precision.HIGHEST)
    velocity = momentum / density[None, :]
    project = jnp.dot(table["vecs"], velocity, precision=lax.Precision.HIGHEST)
    speed_sq = jnp.sum(velocity * velocity, 0)
    equil = (
        table["wvec"][:, None]
        * density[None, :]
        * (1.0 + 3.0 * project + 4.5 * project * project - 1.5 * speed_sq[None, :])
    )
    noneq = flat - equil
    stress = jnp.dot(table["stress"], noneq, precision=lax.Precision.HIGHEST)
    square = jnp.sum(stress[:3] * stress[:3], 0) + 2.0 * jnp.sum(stress[3:] * stress[3:], 0)
    relax_time = 0.5 * (
        TAU_ZERO
        + jnp.sqrt(TAU_ZERO * TAU_ZERO + 18.0 * SMAGORINSKY * jnp.sqrt(square + TINY) / density)
    )
    moments = jnp.dot(table["high"], noneq, precision=lax.Precision.HIGHEST)
    relaxed = jnp.dot(
        table["second"], moments[:6] / relax_time[None, :], precision=lax.Precision.HIGHEST
    )
    relaxed = relaxed + jnp.dot(table["ghost"], moments[6:], precision=lax.Precision.HIGHEST)
    return flat - relaxed + table["push"][:, None] * force[None, :]


def wall_mask(vectors, depth):
    keep = np.ones((19, depth))
    for column in range(19):
        if vectors[column, 2] > 0.5:
            keep[column, 0] = 0.0
        if vectors[column, 2] < -0.5:
            keep[column, depth - 1] = 0.0
    return keep


def neighbours(field, vectors, direction):
    pops, width_x, span = field.shape
    depth = NZ
    width_y = span // depth
    step_x = [int(direction * vectors[column, 0]) for column in range(19)]
    step_y = [int(direction * vectors[column, 1]) for column in range(19)]
    step_z = [int(direction * vectors[column, 2]) for column in range(19)]
    padded = extended(field.reshape(pops, width_x, width_y, depth), (("gx", 1), ("gy", 2)), 1)
    padded = padded.reshape(pops, width_x + 2, (width_y + 2) * depth)
    padded = jnp.pad(padded, ((0, 0), (0, 0), (1, 1)))
    pieces = []
    for column in range(19):
        start_x = 1 - step_x[column]
        start_j = depth + 1 - step_y[column] * depth - step_z[column]
        pieces.append(padded[column, start_x : start_x + width_x, start_j : start_j + span])
    return jnp.stack(pieces, 0)


def turbine_total(partial_value):
    return lax.psum(partial_value, ("gx", "gy"))


def body(checkpoint, cotangent, blade_area, hub_tile, point_side, point_local):
    table = tables()
    vectors = table["vectors"]
    opposite = table["opposite"]
    pops, width_x, span = checkpoint.shape
    width_y = span // NZ
    cells = width_x * span
    keep = jnp.asarray(np.tile(wall_mask(vectors, NZ), (1, width_y)), jnp.float32)[:, None, :]
    count_x = lax.axis_size("gx")
    count_y = lax.axis_size("gy")
    index_x = lax.axis_index("gx")
    index_y = lax.axis_index("gy")
    turbine = jnp.arange(NTURB * PTS, dtype=jnp.int32) // PTS
    hub_x = hub_tile // count_y
    hub_y = hub_tile % count_y
    tile_x = (hub_x[turbine] + point_side // 3 - 1) % count_x
    tile_y = (hub_y[turbine] + point_side % 3 - 1) % count_y
    mine = ((tile_x == index_x) & (tile_y == index_y)).astype(jnp.float32)
    denom = jnp.sum(blade_area.reshape(NTURB, PTS), 1)

    def stream_adjoint(adjoint):
        pushed = neighbours(adjoint * keep, vectors, -1)
        return pushed + ((1.0 - keep) * adjoint)[opposite]

    def collide_local(flat, force):
        return collide(flat, force, table)

    def velocity_local(flat):
        return streamwise_velocity(flat, table)

    field = checkpoint
    saved = []
    for counter in range(STEPS):
        flat = (neighbours(field, vectors, 1) * keep + (1.0 - keep) * field[opposite]).reshape(
            pops, cells
        )
        sampled = velocity_local(flat)[point_local] * mine
        numer = turbine_total(jnp.sum((blade_area * sampled).reshape(NTURB, PTS), 1))
        rotor = numer / denom
        thrust = -THRUST * blade_area * rotor[turbine] * sampled
        force = jnp.zeros((cells,), jnp.float32).at[point_local].add(thrust)
        saved.append((flat, sampled, rotor, force))
        field = collide_local(flat, force).reshape(pops, width_x, span)
    adjoint = cotangent
    area_grad = jnp.zeros_like(blade_area)
    for counter in range(STEPS - 1, -1, -1):
        flat, sampled, rotor, force = saved[counter]
        unused, pullback = jax.vjp(collide_local, flat, force)
        flat_bar, force_bar = pullback(adjoint.reshape(pops, cells))
        thrust_bar = force_bar[point_local] * mine
        rotor_here = rotor[turbine]
        sample_bar = thrust_bar * -THRUST * blade_area * rotor_here
        rotor_part = jnp.sum((thrust_bar * -THRUST * blade_area * sampled).reshape(NTURB, PTS), 1)
        rotor_bar = turbine_total(rotor_part)
        numer_bar = rotor_bar / denom
        sample_bar = sample_bar + numer_bar[turbine] * blade_area * mine
        area_grad = area_grad + thrust_bar * -THRUST * rotor_here * sampled
        area_grad = area_grad + mine * rotor_bar[turbine] * (sampled - rotor_here) / denom[turbine]
        speed_bar = jnp.zeros((cells,), jnp.float32).at[point_local].add(sample_bar)
        unused_speed, speed_pull = jax.vjp(velocity_local, flat)
        flat_bar = flat_bar + speed_pull(speed_bar)[0]
        adjoint = stream_adjoint(flat_bar.reshape(pops, width_x, span))
    grad_area = lax.psum(area_grad, ("gx", "gy"))
    return (adjoint, grad_area)


def solution(mesh):
    return jax.shard_map(
        body,
        mesh=mesh,
        in_specs=(P(None, "gx", "gy"), P(None, "gx", "gy"), P(), P(), P(), P()),
        out_specs=(P(None, "gx", "gy"), P()),
        check_vma=False,
    )
```

profile of v0, /device:TPU:1, one launch (start us, length us, event | category | flops | bytes accessed | tf_op | source)
XLA Modules:
  0.0 1147.3 jit_solution(11894280306716798596)
XLA Ops:
  2.0 2.7 collective-permute-start
  7.4 8.9 select_reduce_fusion.13
  18.5 3.0 collective-permute-start.3
  29.9 8.4 gather_fusion.1
  38.4 11.2 fusion.199
  49.9 82.5 %psum.63 = f32[16]{0:T(128)S(1)} all-reduce(f32[16]{0:T(128)S(1)} %reduce_sum.414), channel_id=1, replica_groups=mesh['gx'=32,'gy'=8] {'gx','gy'}, use_global_device_ids=true, to_apply=%region_5.6 | all-reduce | flops 16 | bytes 128 | tf_op jit(solution)/shard_map/psum | solution.py:182
  133.1 4.4 select_reduce_fusion.12
  137.6 5.7 multiply_multiply_fusion.26
  143.3 8.7 scatter_custom_fusion
  156.2 2.4 collective-permute-done.5
  159.3 3.2 collective-permute-start.7
  172.3 8.4 gather_fusion.3
  181.3 84.2 %psum.64 = f32[16]{0:T(128)S(1)} all-reduce(f32[16]{0:T(128)S(1)} %reduce_sum.426), channel_id=1, replica_groups=mesh['gx'=32,'gy'=8] {'gx','gy'}, use_global_device_ids=true, to_apply=%region_13.14 | all-reduce | flops 16 | bytes 128 | tf_op jit(solution)/shard_map/psum | solution.py:182
  266.3 4.4 select_reduce_fusion.11
  270.7 5.7 multiply_multiply_fusion.25
  276.4 8.8 scatter_custom_fusion.1
  288.8 3.3 collective-permute-done.9
  293.3 2.8 collective-permute-start.11
  305.6 8.4 gather_fusion.5
  314.6 84.7 %psum.65 = f32[16]{0:T(128)S(1)} all-reduce(f32[16]{0:T(128)S(1)} %reduce_sum.434), channel_id=1, replica_groups=mesh['gx'=32,'gy'=8] {'gx','gy'}, use_global_device_ids=true, to_apply=%region_20.21 | all-reduce | flops 16 | bytes 128 | tf_op jit(solution)/shard_map/psum | solution.py:182
  400.0 4.5 select_reduce_fusion.10
  404.6 5.7 multiply_multiply_fusion.24
  410.3 8.8 scatter_custom_fusion.2
  421.1 11.7 %gather_fusion.7 = f32[1536]{0:T(1024)} fusion(f32[2048]{0:T(1024)S(1)} %bitcast.826, s32[2048]{0:T(1024)S(1)} %copy-done.21), kind=kCustom, calls=%fused_computation.7 | custom fusion | bytes 18432 | tf_op jit(solution)/shard_map/gather | solution.py:234
  433.9 3.5 collective-permute-done.13
  439.3 3.3 collective-permute-start.15
  442.6 5.1 select_reduce_fusion.3
  455.5 8.4 gather_fusion.8
  465.3 81.7 %all-reduce.28 = (f32[16]{0:T(128)S(1)}, f32[16]{0:T(128)S(1)}) all-reduce(f32[16]{0:T(128)S(1)} %reduce_sum.455, f32[16]{0:T(128)S(1)} %reduce_sum.454), channel_id=1, replica_groups=mesh['gx'=32,'gy'=8] {'gx','gy'}, use_global_device_ids=true, to_apply=%region_34.35 | all-reduce | flops 32 | bytes 256 | tf_op jit(solution)/shard_map/psum | solution.py:182
  548.4 4.4 select_reduce_fusion.9
  552.9 4.5 select_reduce_fusion.8
  557.5 11.6 %fusion.186 = f32[1536]{0:T(1024)S(1)} fusion(pred[1536]{0:T(1024)(128)(4,1)S(1)} %copy-done.69, f32[1536]{0:T(1024)S(1)} %copy-done.5, pred[1536]{0:T(1024)(128)(4,1)S(1)} %copy-done.76, pred[1536]{0:T(1024)(128)(4,1)S(1)} %copy-done.84, pred[1536]{0:T(1024)(128)(4,1)S(1)} %copy-done.92, pred[1536]{0:T(1024)(128)(4,1)S(1)} %copy-done.100, ...), kind=kLoop, calls=%fused_computation.541 | loop fusion | flops 38400 | bytes 46152 | tf_op jit(solution)/shard_map/add | solution.py:240
  569.1 8.8 scatter_custom_fusion.3
  583.4 2.5 collective-permute-done.17
  586.1 3.9 collective-permute-start.19
  590.1 5.1 select_reduce_fusion.4
  597.0 2.2 reshape.1667
  600.7 8.4 gather_fusion.10
  609.6 80.4 %psum.68 = f32[16]{0:T(128)S(1)} all-reduce(f32[16]{0:T(128)S(1)} %reduce_sum.468), channel_id=1, replica_groups=mesh['gx'=32,'gy'=8] {'gx','gy'}, use_global_device_ids=true, to_apply=%region_42.43 | all-reduce | flops 16 | bytes 128 | tf_op jit(solution)/shard_map/psum | solution.py:182
  693.2 4.3 select_reduce_fusion.7
  697.6 11.3 fusion.184
  708.9 8.8 scatter_custom_fusion.4
  722.9 2.5 collective-permute-done.21
  725.6 3.7 collective-permute-start.23
  729.3 5.0 select_reduce_fusion.2
  736.2 2.2 reshape.1668
  739.8 8.4 gather_fusion.12
  748.6 80.9 %psum.69 = f32[16]{0:T(128)S(1)} all-reduce(f32[16]{0:T(128)S(1)} %reduce_sum.478), channel_id=1, replica_groups=mesh['gx'=32,'gy'=8] {'gx','gy'}, use_global_device_ids=true, to_apply=%region_50.51 | all-reduce | flops 16 | bytes 128 | tf_op jit(solution)/shard_map/psum | solution.py:182
  832.7 4.4 select_reduce_fusion.6
  837.3 11.3 fusion.182
  848.6 8.8 scatter_custom_fusion.5
  862.3 2.5 collective-permute-done.25
  865.0 3.8 collective-permute-start.27
  868.8 5.0 select_reduce_fusion.1
  879.3 8.4 gather_fusion.14
  888.2 81.0 %psum.70 = f32[16]{0:T(128)S(1)} all-reduce(f32[16]{0:T(128)S(1)} %reduce_sum.491), channel_id=1, replica_groups=mesh['gx'=32,'gy'=8] {'gx','gy'}, use_global_device_ids=true, to_apply=%region_58.59 | all-reduce | flops 16 | bytes 128 | tf_op jit(solution)/shard_map/psum | solution.py:182
  972.4 4.4 select_reduce_fusion.5
  977.0 11.2 fusion.180
  988.2 8.8 scatter_custom_fusion.6
  1000.9 4.5 select_reduce_fusion
  1005.9 3.4 collective-permute-start.31
  1009.5 50.7 %fusion.166 = f32[1536]{0:T(1024)S(1)} fusion(pred[1536]{0:T(1024)(128)(4,1)S(1)} %copy-done.72, pred[1536]{0:T(1024)(128)(4,1)S(1)} %copy-done.80, pred[1536]{0:T(1024)(128)(4,1)S(1)} %copy-done.88, pred[1536]{0:T(1024)(128)(4,1)S(1)} %copy-done.96, pred[1536]{0:T(1024)(128)(4,1)S(1)} %copy-done.104, pred[1536]{0:T(1024)(128)(4,1)S(1)} %copy-done.112, ...), kind=kLoop, calls=%fused_computation.513 | loop fusion | flops 190464 | bytes 126276 | tf_op jit(solution)/shard_map/add | solution.py:242
  1061.0 80.0 %psum.71 = f32[1536]{0:T(1024)} all-reduce(f32[1536]{0:T(1024)S(1)} %fusion.166), channel_id=1, replica_groups=mesh['gx'=32,'gy'=8] {'gx','gy'}, use_global_device_ids=true, to_apply=%region_60.61 | all-reduce | flops 1536 | bytes 12288 | tf_op jit(solution)/shard_map/psum | solution.py:247
  1142.8 2.2 reshape.1670
  (1152 shorter events, 106.0 us)
Async XLA Ops:
  2.0 14.3 %collective-permute-start = (f32[19,1,16,16]{3,2,1,0:T(8,128)S(1)}, f32[19,1,16,16]{3,2,1,0:T(8,128)S(1)}, u32[]{:S(2)}, u32[]{:S(2)}) collective-permute-start(f32[19,1,16,16]{3,2,1,0:T(8,128)S(1)} %get-tuple-element.69), channel_id=1, source_target_pairs={{0,8},{8,16},{16,24},{24,32},{32,40},{40,48},{48,56},{56,64},{64,7... | collective-permute-start | bytes 58376 | tf_op jit(solution)/shard_map/ppermute | solution.py:25
  4.7 11.8 %collective-permute-start.1 = (f32[19,1,16,16]{3,2,1,0:T(8,128)S(1)}, f32[19,1,16,16]{3,2,1,0:T(8,128)S(1)}, u32[]{:S(2)}, u32[]{:S(2)}) collective-permute-start(f32[19,1,16,16]{3,2,1,0:T(8,128)S(1)} %get-tuple-element.68), channel_id=1, source_target_pairs={{8,0},{16,8},{24,16},{32,24},{40,32},{48,40},{56,48},{64,56},{72,6... | collective-permute-start | bytes 58376 | tf_op jit(solution)/shard_map/ppermute | solution.py:26
  5.5 132.0 %copy-start.73 = (pred[1536]{0:T(1024)(128)(4,1)}, pred[1536]{0:T(1024)(128)(4,1)S(1)}, u32[]{:S(2)}) copy-start(pred[1536]{0:T(1024)(128)(4,1)S(1)} %compare_reduce_fusion) | copy-start | bytes 4612
  5.5 132.0 %copy-start.81 = (pred[1536]{0:T(1024)(128)(4,1)}, pred[1536]{0:T(1024)(128)(4,1)S(1)}, u32[]{:S(2)}) copy-start(pred[1536]{0:T(1024)(128)(4,1)S(1)} %compare_reduce_fusion.1) | copy-start | bytes 4612
  5.6 131.9 %copy-start.89 = (pred[1536]{0:T(1024)(128)(4,1)}, pred[1536]{0:T(1024)(128)(4,1)S(1)}, u32[]{:S(2)}) copy-start(pred[1536]{0:T(1024)(128)(4,1)S(1)} %compare_reduce_fusion.2) | copy-start | bytes 4612
  5.7 131.8 %copy-start.97 = (pred[1536]{0:T(1024)(128)(4,1)}, pred[1536]{0:T(1024)(128)(4,1)S(1)}, u32[]{:S(2)}) copy-start(pred[1536]{0:T(1024)(128)(4,1)S(1)} %compare_reduce_fusion.3) | copy-start | bytes 4612
  5.8 131.8 %copy-start.105 = (pred[1536]{0:T(1024)(128)(4,1)}, pred[1536]{0:T(1024)(128)(4,1)S(1)}, u32[]{:S(2)}) copy-start(pred[1536]{0:T(1024)(128)(4,1)S(1)} %compare_reduce_fusion.4) | copy-start | bytes 4612
  5.8 131.7 %copy-start.113 = (pred[1536]{0:T(1024)(128)(4,1)}, pred[1536]{0:T(1024)(128)(4,1)S(1)}, u32[]{:S(2)}) copy-start(pred[1536]{0:T(1024)(128)(4,1)S(1)} %compare_reduce_fusion.5) | copy-start | bytes 4612
  5.9 137.3 %copy-start.255 = (s32[1536]{0:T(1024)}, s32[1536]{0:T(1024)S(1)}, u32[]{:S(2)}) copy-start(s32[1536]{0:T(1024)S(1)} %compare_select_fusion.1) | copy-start | bytes 18436
  7.4 130.1 %copy-start.121 = (pred[1536]{0:T(1024)(128)(4,1)}, pred[1536]{0:T(1024)(128)(4,1)S(1)}, u32[]{:S(2)}) copy-start(pred[1536]{0:T(1024)(128)(4,1)S(1)} %compare_reduce_fusion.6) | copy-start | bytes 4612
  17.8 5.6 collective-permute-start.2
  18.5 5.0 collective-permute-start.3
  21.5 116.0 %copy-start.129 = (pred[1536]{0:T(1024)(128)(4,1)}, pred[1536]{0:T(1024)(128)(4,1)S(1)}, u32[]{:S(2)}) copy-start(pred[1536]{0:T(1024)(128)(4,1)S(1)} %compare_reduce_fusion.7) | copy-start | bytes 4612
  22.4 115.2 %copy-start.137 = (pred[1536]{0:T(1024)(128)(4,1)}, pred[1536]{0:T(1024)(128)(4,1)S(1)}, u32[]{:S(2)}) copy-start(pred[1536]{0:T(1024)(128)(4,1)S(1)} %compare_reduce_fusion.8) | copy-start | bytes 4612
  27.9 124.0 %copy-start.52 = (f32[1,2,8,128]{3,1,2,0:T(2,128)}, f32[1,2,8,128]{3,1,2,0:T(2,128)S(1)}, u32[]{:S(2)}) copy-start(f32[1,2,8,128]{3,1,2,0:T(2,128)S(1)} %copy.360) | copy-start | bytes 24580
  28.8 123.1 %copy-start.212 = (f32[2048]{0:T(1024)}, f32[2048]{0:T(1024)S(1)}, u32[]{:S(2)}) copy-start(f32[2048]{0:T(1024)S(1)} %broadcast_multiply_fusion.15) | copy-start | bytes 24580
  29.9 122.4 %copy-start.218 = (f32[2048]{0:T(1024)}, f32[2048]{0:T(1024)S(1)}, u32[]{:S(2)}) copy-start(f32[2048]{0:T(1024)S(1)} %get-tuple-element.23) | copy-start | bytes 24580
  29.9 122.0 %copy-start.59 = (f32[15,19]{1,0:T(8,128)S(1)}, f32[15,19]{1,0:T(8,128)}, u32[]{:S(2)}) copy-start(f32[15,19]{1,0:T(8,128)} %constant.153.clone) | copy-start | bytes 3424
  29.9 122.4 %copy-start.34 = (f32[19,6]{1,0:T(8,128)S(1)}, f32[19,6]{1,0:T(8,128)}, u32[]{:S(2)}) copy-start(f32[19,6]{1,0:T(8,128)} %constant.154.clone) | copy-start | bytes 1372
  29.9 122.7 %copy-start.40 = (f32[19,9]{1,0:T(8,128)S(1)}, f32[19,9]{1,0:T(8,128)}, u32[]{:S(2)}) copy-start(f32[19,9]{1,0:T(8,128)} %constant.155.clone) | copy-start | bytes 2056
  29.9 122.7 %copy-start.263 = (f32[19]{0:T(128)S(1)}, f32[19]{0:T(128)}, u32[]{:S(2)}) copy-start(f32[19]{0:T(128)} %constant.157.clone) | copy-start | bytes 232
  38.4 113.9 %copy-start.145 = (f32[1536]{0:T(1024)}, f32[1536]{0:T(1024)S(1)}, u32[]{:S(2)}) copy-start(f32[1536]{0:T(1024)S(1)} %gather_fusion.1) | copy-start | bytes 18436
  49.6 103.1 %copy-start.66 = (pred[1536]{0:T(1024)(128)(4,1)}, pred[1536]{0:T(1024)(128)(4,1)S(1)}, u32[]{:S(2)}) copy-start(pred[1536]{0:T(1024)(128)(4,1)S(1)} %get-tuple-element.37) | copy-start | bytes 4612
  153.5 2.6 collective-permute-start.4
  153.9 4.7 collective-permute-start.5
  158.8 6.6 collective-permute-start.6
  159.3 6.1 collective-permute-start.7
  172.1 113.1 %copy-start.220 = (f32[2048]{0:T(1024)}, f32[2048]{0:T(1024)S(1)}, u32[]{:S(2)}) copy-start(f32[2048]{0:T(1024)S(1)} %get-tuple-element.27) | copy-start | bytes 24580
  172.2 113.0 %copy-start.35 = (f32[19,6]{1,0:T(8,128)S(1)}, f32[19,6]{1,0:T(8,128)}, u32[]{:S(2)}) copy-start(f32[19,6]{1,0:T(8,128)} %constant.154.clone) | copy-start | bytes 1372
  172.2 113.3 %copy-start.41 = (f32[19,9]{1,0:T(8,128)S(1)}, f32[19,9]{1,0:T(8,128)}, u32[]{:S(2)}) copy-start(f32[19,9]{1,0:T(8,128)} %constant.155.clone) | copy-start | bytes 2056
  172.3 113.3 %copy-start.264 = (f32[19]{0:T(128)S(1)}, f32[19]{0:T(128)}, u32[]{:S(2)}) copy-start(f32[19]{0:T(128)} %constant.157.clone) | copy-start | bytes 232
  180.7 104.8 %copy-start.148 = (f32[1536]{0:T(1024)}, f32[1536]{0:T(1024)S(1)}, u32[]{:S(2)}) copy-start(f32[1536]{0:T(1024)S(1)} %gather_fusion.3) | copy-start | bytes 18436
  181.3 104.2 %copy-start.15 = (f32[15,2048]{1,0:T(8,128)}, f32[15,2048]{1,0:T(8,128)S(1)}, u32[]{:S(2)}) copy-start(f32[15,2048]{1,0:T(8,128)S(1)} %fusion.261) | copy-start | bytes 368644
  286.4 2.3 collective-permute-start.8
  287.4 4.7 collective-permute-start.9
  292.2 6.5 collective-permute-start.10
  293.3 5.4 collective-permute-start.11
  305.5 113.6 %copy-start.222 = (f32[2048]{0:T(1024)}, f32[2048]{0:T(1024)S(1)}, u32[]{:S(2)}) copy-start(f32[2048]{0:T(1024)S(1)} %get-tuple-element.31) | copy-start | bytes 24580
  305.6 113.5 %copy-start.36 = (f32[19,6]{1,0:T(8,128)S(1)}, f32[19,6]{1,0:T(8,128)}, u32[]{:S(2)}) copy-start(f32[19,6]{1,0:T(8,128)} %constant.154.clone) | copy-start | bytes 1372
  305.6 113.9 %copy-start.42 = (f32[19,9]{1,0:T(8,128)S(1)}, f32[19,9]{1,0:T(8,128)}, u32[]{:S(2)}) copy-start(f32[19,9]{1,0:T(8,128)} %constant.155.clone) | copy-start | bytes 2056
  305.6 113.9 %copy-start.266 = (f32[19]{0:T(128)S(1)}, f32[19]{0:T(128)}, u32[]{:S(2)}) copy-start(f32[19]{0:T(128)} %constant.157.clone) | copy-start | bytes 232
  314.1 105.4 %copy-start.151 = (f32[1536]{0:T(1024)}, f32[1536]{0:T(1024)S(1)}, u32[]{:S(2)}) copy-start(f32[1536]{0:T(1024)S(1)} %gather_fusion.5) | copy-start | bytes 18436
  314.6 104.8 %copy-start.17 = (f32[15,2048]{1,0:T(8,128)}, f32[15,2048]{1,0:T(8,128)S(1)}, u32[]{:S(2)}) copy-start(f32[15,2048]{1,0:T(8,128)S(1)} %fusion.257) | copy-start | bytes 368644
  420.3 13.6 %collective-permute-start.12 = (f32[19,1,16,16]{3,2,1,0:T(8,128)S(1)}, f32[19,1,16,16]{3,2,1,0:T(8,128)S(1)}, u32[]{:S(2)}, u32[]{:S(2)}) collective-permute-start(f32[19,1,16,16]{3,2,1,0:T(8,128)S(1)} %get-tuple-element.63), channel_id=1, source_target_pairs={{0,8},{8,16},{16,24},{24,32},{32,40},{40,48},{48,56},{56,64},{64,7... | collective-permute-start | bytes 58376 | tf_op jit(solution)/shard_map/ppermute | solution.py:25
  432.8 4.7 collective-permute-start.13
  438.8 10.4 collective-permute-start.14
  439.3 9.9 collective-permute-start.15
  463.9 114.8 %copy-start.232 = (f32[1536]{0:T(1024)}, f32[1536]{0:T(1024)S(1)}, u32[]{:S(2)}) copy-start(f32[1536]{0:T(1024)S(1)} %gather_fusion.8) | copy-start | bytes 18436
  579.7 3.6 collective-permute-start.16
  581.2 4.7 collective-permute-start.17
  586.0 9.1 collective-permute-start.18
  586.1 9.0 collective-permute-start.19
  719.5 3.4 collective-permute-start.20
  720.7 4.7 collective-permute-start.21
  725.5 8.8 collective-permute-start.22
  725.6 8.7 collective-permute-start.23
  859.2 3.1 collective-permute-start.24
  860.1 4.7 collective-permute-start.25
  865.0 8.9 collective-permute-start.26
  865.0 8.8 collective-permute-start.27
  999.1 6.4 collective-permute-start.28
  1000.1 5.3 collective-permute-start.29
  1005.7 135.3 %collective-permute-start.30 = (f32[19,10,1,16]{3,2,1,0:T(1,128)S(1)}, f32[19,10,1,16]{3,2,1,0:T(1,128)S(1)}, u32[]{:S(2)}, u32[]{:S(2)}) collective-permute-start(f32[19,10,1,16]{3,2,1,0:T(1,128)S(1)} %get-tuple-element.38), channel_id=1, source_target_pairs={{0,1},{1,2},{2,3},{3,4},{4,5},{5,6},{6,7},{7,0},{8,9},{9,10},{10,1... | collective-permute-start | bytes 36488 | tf_op jit(solution)/shard_map/ppermute | solution.py:25
  1005.9 135.1 %collective-permute-start.31 = (f32[19,10,1,16]{3,2,1,0:T(1,128)S(1)}, f32[19,10,1,16]{3,2,1,0:T(1,128)S(1)}, u32[]{:S(2)}, u32[]{:S(2)}) collective-permute-start(f32[19,10,1,16]{3,2,1,0:T(1,128)S(1)} %get-tuple-element.39), channel_id=1, source_target_pairs={{1,0},{2,1},{3,2},{4,3},{5,4},{6,5},{7,6},{0,7},{9,8},{10,9},{11,1... | collective-permute-start | bytes 36488 | tf_op jit(solution)/shard_map/ppermute | solution.py:26
  (243 other events, 7864.3 us)
where the time goes:
time: 1160 us; the launch traced here: 1150 us
  blocking collectives  655 us (56%)
  other arithmetic  277 us (24%)
  local copies, waits for them, and re-layouts  125 us (11%)
  starting transfers between devices  41.8 us (4%)
  waiting for transfers between devices  23 us (2%)
  matrix products  17.3 us (1%)
    psum x7, blocking collectives, turbine_total(): return lax.psum(partial_value, ('gx', 'gy'))  575 us
    psum x1, blocking collectives, body(): grad_area = lax.psum(area_grad, ('gx', 'gy'))  80 us
    add x1, other arithmetic, body(): area_grad + mine * rotor_bar[turbine] * (sampled - rotor_here) / denom[tu...  50.7 us
    add x4, other arithmetic, body(): sample_bar = sample_bar + numer_bar[turbine] * blade_area * mine  45.4 us
    gather x4, local copies, waits for them, and re-layouts, body(): thrust_bar = force_bar[point_local] * mine  36.9 us
    scatter-add x4, other arithmetic, body(): speed_bar = jnp.zeros((cells,), jnp.float32).at[point_local].add(sample_bar)  35.2 us
    gather x4, local copies, waits for them, and re-layouts, body(): sampled = velocity_local(flat)[point_local] * mine  33.6 us
    ppermute x16, starting transfers between devices, extended(): after = lax.ppermute(first, axis, down)  30.8 us
  transfers between devices with their start and end apart: 32, of which 14 were waited for; matrix products, arithmetic and copies ran while one was open for 10% of the time, Pallas kernels for 0%

commit v1 on v0

--- a/solution.py
+++ b/solution.py
@@ -179,7 +179,7 @@
 
 
 def turbine_total(partial_value):
-    return lax.psum(partial_value, ("gx", "gy"))
+    return lax.psum(lax.psum(partial_value, "gy"), "gx")
 
 
 def body(checkpoint, cotangent, blade_area, hub_tile, point_side, point_local):

time: 1160 us -> 1240 us (1.069)
  blocking collectives: 655 us -> 745 us
    psum x7 -> x14, blocking collectives: 575 us -> 664 us  [turbine_total(): return lax.psum(lax.psum(partial_value, 'gy'), 'gx')]
  transfers between devices with their start and end apart: 32 -> 32, of which waited for: 14 -> 10; matrix products, arithmetic and copies ran while one was open for 10% -> 9% of each run, Pallas kernels for 0% -> 0%
where the time goes in v1:
time: 1240 us; the launch traced here: 1230 us
  blocking collectives  745 us (60%)
  other arithmetic  276 us (22%)
  local copies, waits for them, and re-layouts  125 us (10%)
  starting transfers between devices  46.1 us (4%)
  matrix products  17.3 us (1%)
  waiting for transfers between devices  14.9 us (1%)
    psum x14, blocking collectives, turbine_total(): return lax.psum(lax.psum(partial_value, 'gy'), 'gx')  664 us
    psum x1, blocking collectives, body(): grad_area = lax.psum(area_grad, ('gx', 'gy'))  80.3 us
    add x1, other arithmetic, body(): area_grad + mine * rotor_bar[turbine] * (sampled - rotor_here) / denom[tu...  50.4 us
    add x4, other arithmetic, body(): sample_bar = sample_bar + numer_bar[turbine] * blade_area * mine  44.9 us
    ppermute x16, starting transfers between devices, extended(): after = lax.ppermute(first, axis, down)  39.2 us
    gather x4, local copies, waits for them, and re-layouts, body(): thrust_bar = force_bar[point_local] * mine  36.9 us
    scatter-add x4, other arithmetic, body(): speed_bar = jnp.zeros((cells,), jnp.float32).at[point_local].add(sample_bar)  35.2 us
    gather x4, local copies, waits for them, and re-layouts, body(): sampled = velocity_local(flat)[point_local] * mine  33.6 us
  transfers between devices with their start and end apart: 32, of which 10 were waited for; matrix products, arithmetic and copies ran while one was open for 9% of the time, Pallas kernels for 0%

profile of v1, /device:TPU:1, one launch (start us, length us, event | category | flops | bytes accessed | tf_op | source)
XLA Modules:
  0.0 1231.5 jit_solution(56798369825196747)
XLA Ops:
  2.0 2.7 collective-permute-start
  7.5 8.8 select_reduce_fusion.13
  18.4 3.0 collective-permute-start.3
  29.9 8.4 gather_fusion.1
  38.4 11.3 fusion.199
  49.9 16.0 %psum.119 = f32[16]{0:T(128)S(1)} all-reduce(f32[16]{0:T(128)S(1)} %reduce_sum.414), channel_id=1, replica_groups=mesh['gx'=32,'gy'=8] {'gy'}, use_global_device_ids=true, to_apply=%region_5.6 | all-reduce | flops 16 | bytes 128 | tf_op jit(solution)/shard_map/psum | solution.py:182
  65.9 80.6 %psum.120 = f32[16]{0:T(128)S(1)} all-reduce(f32[16]{0:T(128)S(1)} %psum.119), channel_id=1, replica_groups=mesh['gx'=32,'gy'=8] {'gx'}, use_global_device_ids=true, to_apply=%region_6.7 | all-reduce | flops 16 | bytes 128 | tf_op jit(solution)/shard_map/psum | solution.py:182
  147.3 4.5 select_reduce_fusion.12
  151.8 5.5 multiply_multiply_fusion.26
  157.4 8.7 scatter_custom_fusion
  172.8 3.6 collective-permute-start.7
  185.7 8.4 gather_fusion.3
  194.3 16.1 %psum.121 = f32[16]{0:T(128)S(1)} all-reduce(f32[16]{0:T(128)S(1)} %reduce_sum.426), channel_id=1, replica_groups=mesh['gx'=32,'gy'=8] {'gy'}, use_global_device_ids=true, to_apply=%region_14.15 | all-reduce | flops 16 | bytes 128 | tf_op jit(solution)/shard_map/psum | solution.py:182
  210.5 80.8 %psum.122 = f32[16]{0:T(128)S(1)} all-reduce(f32[16]{0:T(128)S(1)} %psum.121), channel_id=1, replica_groups=mesh['gx'=32,'gy'=8] {'gx'}, use_global_device_ids=true, to_apply=%region_15.16 | all-reduce | flops 16 | bytes 128 | tf_op jit(solution)/shard_map/psum | solution.py:182
  292.0 4.5 select_reduce_fusion.11
  296.6 5.5 multiply_multiply_fusion.25
  302.1 8.8 scatter_custom_fusion.1
  315.2 2.7 collective-permute-done.9
  318.1 3.8 collective-permute-start.11
  331.8 8.4 gather_fusion.5
  340.5 15.4 %psum.123 = f32[16]{0:T(128)S(1)} all-reduce(f32[16]{0:T(128)S(1)} %reduce_sum.434), channel_id=1, replica_groups=mesh['gx'=32,'gy'=8] {'gy'}, use_global_device_ids=true, to_apply=%region_22.23 | all-reduce | flops 16 | bytes 128 | tf_op jit(solution)/shard_map/psum | solution.py:182
  355.9 81.3 %psum.124 = f32[16]{0:T(128)S(1)} all-reduce(f32[16]{0:T(128)S(1)} %psum.123), channel_id=1, replica_groups=mesh['gx'=32,'gy'=8] {'gx'}, use_global_device_ids=true, to_apply=%region_23.24 | all-reduce | flops 16 | bytes 128 | tf_op jit(solution)/shard_map/psum | solution.py:182
  437.9 4.4 select_reduce_fusion.10
  442.5 5.6 multiply_multiply_fusion.24
  448.1 8.8 scatter_custom_fusion.2
  458.9 11.8 gather_fusion.7
  472.4 2.9 collective-permute-done.13
  476.7 3.9 collective-permute-start.15
  480.7 5.1 select_reduce_fusion.3
  493.5 8.4 gather_fusion.8
  503.3 12.5 %all-reduce.29 = (f32[16]{0:T(128)S(1)}, f32[16]{0:T(128)S(1)}) all-reduce(f32[16]{0:T(128)S(1)} %reduce_sum.455, f32[16]{0:T(128)S(1)} %reduce_sum.454), channel_id=1, replica_groups=mesh['gx'=32,'gy'=8] {'gy'}, use_global_device_ids=true, to_apply=%region_38.39 | all-reduce | flops 32 | bytes 256 | tf_op jit(solution)/shard_map/psum | solution.py:182
  515.8 79.2 %all-reduce.28 = (f32[16]{0:T(128)S(1)}, f32[16]{0:T(128)S(1)}) all-reduce(f32[16]{0:T(128)S(1)} %get-tuple-element.20, f32[16]{0:T(128)S(1)} %get-tuple-element.21), channel_id=1, replica_groups=mesh['gx'=32,'gy'=8] {'gx'}, use_global_device_ids=true, to_apply=%region_39.40 | all-reduce | flops 32 | bytes 256 | tf_op jit(solution)/shard_map/psum | solution.py:182
  596.4 4.3 select_reduce_fusion.9
  600.7 4.4 select_reduce_fusion.8
  605.2 11.3 fusion.186
  616.5 8.8 scatter_custom_fusion.3
  627.2 2.6 collective-permute-start.17
  635.9 4.9 select_reduce_fusion.4
  646.4 8.4 gather_fusion.10
  655.2 13.1 %psum.129 = f32[16]{0:T(128)S(1)} all-reduce(f32[16]{0:T(128)S(1)} %reduce_sum.468), channel_id=1, replica_groups=mesh['gx'=32,'gy'=8] {'gy'}, use_global_device_ids=true, to_apply=%region_47.48 | all-reduce | flops 16 | bytes 128 | tf_op jit(solution)/shard_map/psum | solution.py:182
  668.3 81.8 %psum.130 = f32[16]{0:T(128)S(1)} all-reduce(f32[16]{0:T(128)S(1)} %psum.129), channel_id=1, replica_groups=mesh['gx'=32,'gy'=8] {'gx'}, use_global_device_ids=true, to_apply=%region_48.49 | all-reduce | flops 16 | bytes 128 | tf_op jit(solution)/shard_map/psum | solution.py:182
  753.3 4.3 select_reduce_fusion.7
  757.7 11.3 fusion.184
  769.0 8.8 scatter_custom_fusion.4
  784.7 3.8 collective-permute-start.23
  788.5 5.0 select_reduce_fusion.2
  799.0 8.4 gather_fusion.12
  807.7 13.0 %psum.131 = f32[16]{0:T(128)S(1)} all-reduce(f32[16]{0:T(128)S(1)} %reduce_sum.478), channel_id=1, replica_groups=mesh['gx'=32,'gy'=8] {'gy'}, use_global_device_ids=true, to_apply=%region_56.57 | all-reduce | flops 16 | bytes 128 | tf_op jit(solution)/shard_map/psum | solution.py:182
  820.8 80.8 %psum.132 = f32[16]{0:T(128)S(1)} all-reduce(f32[16]{0:T(128)S(1)} %psum.131), channel_id=1, replica_groups=mesh['gx'=32,'gy'=8] {'gx'}, use_global_device_ids=true, to_apply=%region_57.58 | all-reduce | flops 16 | bytes 128 | tf_op jit(solution)/shard_map/psum | solution.py:182
  904.7 4.4 select_reduce_fusion.6
  909.2 11.2 fusion.182
  920.4 8.8 scatter_custom_fusion.5
  936.1 3.8 collective-permute-start.27
  939.9 5.0 select_reduce_fusion.1
  950.4 8.4 gather_fusion.14
  959.2 13.0 %psum.133 = f32[16]{0:T(128)S(1)} all-reduce(f32[16]{0:T(128)S(1)} %reduce_sum.491), channel_id=1, replica_groups=mesh['gx'=32,'gy'=8] {'gy'}, use_global_device_ids=true, to_apply=%region_65.66 | all-reduce | flops 16 | bytes 128 | tf_op jit(solution)/shard_map/psum | solution.py:182
  972.2 80.7 %psum.134 = f32[16]{0:T(128)S(1)} all-reduce(f32[16]{0:T(128)S(1)} %psum.133), channel_id=1, replica_groups=mesh['gx'=32,'gy'=8] {'gx'}, use_global_device_ids=true, to_apply=%region_66.67 | all-reduce | flops 16 | bytes 128 | tf_op jit(solution)/shard_map/psum | solution.py:182
  1056.1 4.4 select_reduce_fusion.5
  1060.6 11.1 fusion.180
  1071.7 8.8 scatter_custom_fusion.6
  1085.1 4.5 select_reduce_fusion
  1090.8 2.6 collective-permute-start.31
  1093.7 50.4 %fusion.166 = f32[1536]{0:T(1024)S(1)} fusion(pred[1536]{0:T(1024)(128)(4,1)S(1)} %copy-done.73, pred[1536]{0:T(1024)(128)(4,1)S(1)} %copy-done.81, pred[1536]{0:T(1024)(128)(4,1)S(1)} %copy-done.89, pred[1536]{0:T(1024)(128)(4,1)S(1)} %copy-done.97, pred[1536]{0:T(1024)(128)(4,1)S(1)} %copy-done.105, pred[1536]{0:T(1024)(128)(4,1)S(1)} %copy-done.113, ...), kind=kLoop, calls=%fused_computation.513 | loop fusion | flops 190464 | bytes 126276 | tf_op jit(solution)/shard_map/add | solution.py:242
  1144.8 80.3 %psum.135 = f32[1536]{0:T(1024)} all-reduce(f32[1536]{0:T(1024)S(1)} %fusion.166), channel_id=1, replica_groups=mesh['gx'=32,'gy'=8] {'gx','gy'}, use_global_device_ids=true, to_apply=%region_68.69 | all-reduce | flops 1536 | bytes 12288 | tf_op jit(solution)/shard_map/psum | solution.py:247
  (1161 shorter events, 120.0 us)
Async XLA Ops:
  2.0 14.3 %collective-permute-start = (f32[19,1,16,16]{3,2,1,0:T(8,128)S(1)}, f32[19,1,16,16]{3,2,1,0:T(8,128)S(1)}, u32[]{:S(2)}, u32[]{:S(2)}) collective-permute-start(f32[19,1,16,16]{3,2,1,0:T(8,128)S(1)} %get-tuple-element.71), channel_id=1, source_target_pairs={{0,8},{8,16},{16,24},{24,32},{32,40},{40,48},{48,56},{56,64},{64,7... | collective-permute-start | bytes 58376 | tf_op jit(solution)/shard_map/ppermute | solution.py:25
  4.7 11.8 collective-permute-start.1
  5.5 146.3 %copy-start.74 = (pred[1536]{0:T(1024)(128)(4,1)}, pred[1536]{0:T(1024)(128)(4,1)S(1)}, u32[]{:S(2)}) copy-start(pred[1536]{0:T(1024)(128)(4,1)S(1)} %compare_reduce_fusion) | copy-start | bytes 4612
  5.5 146.2 %copy-start.82 = (pred[1536]{0:T(1024)(128)(4,1)}, pred[1536]{0:T(1024)(128)(4,1)S(1)}, u32[]{:S(2)}) copy-start(pred[1536]{0:T(1024)(128)(4,1)S(1)} %compare_reduce_fusion.1) | copy-start | bytes 4612
  5.6 146.2 %copy-start.90 = (pred[1536]{0:T(1024)(128)(4,1)}, pred[1536]{0:T(1024)(128)(4,1)S(1)}, u32[]{:S(2)}) copy-start(pred[1536]{0:T(1024)(128)(4,1)S(1)} %compare_reduce_fusion.2) | copy-start | bytes 4612
  5.7 146.1 %copy-start.98 = (pred[1536]{0:T(1024)(128)(4,1)}, pred[1536]{0:T(1024)(128)(4,1)S(1)}, u32[]{:S(2)}) copy-start(pred[1536]{0:T(1024)(128)(4,1)S(1)} %compare_reduce_fusion.3) | copy-start | bytes 4612
  5.8 146.0 %copy-start.106 = (pred[1536]{0:T(1024)(128)(4,1)}, pred[1536]{0:T(1024)(128)(4,1)S(1)}, u32[]{:S(2)}) copy-start(pred[1536]{0:T(1024)(128)(4,1)S(1)} %compare_reduce_fusion.4) | copy-start | bytes 4612
  5.8 146.0 %copy-start.114 = (pred[1536]{0:T(1024)(128)(4,1)}, pred[1536]{0:T(1024)(128)(4,1)S(1)}, u32[]{:S(2)}) copy-start(pred[1536]{0:T(1024)(128)(4,1)S(1)} %compare_reduce_fusion.5) | copy-start | bytes 4612
  5.9 151.5 %copy-start.256 = (s32[1536]{0:T(1024)}, s32[1536]{0:T(1024)S(1)}, u32[]{:S(2)}) copy-start(s32[1536]{0:T(1024)S(1)} %compare_select_fusion.1) | copy-start | bytes 18436
  7.5 144.4 %copy-start.122 = (pred[1536]{0:T(1024)(128)(4,1)}, pred[1536]{0:T(1024)(128)(4,1)S(1)}, u32[]{:S(2)}) copy-start(pred[1536]{0:T(1024)(128)(4,1)S(1)} %compare_reduce_fusion.6) | copy-start | bytes 4612
  17.8 5.6 collective-permute-start.2
  18.4 5.0 collective-permute-start.3
  21.5 130.3 %copy-start.130 = (pred[1536]{0:T(1024)(128)(4,1)}, pred[1536]{0:T(1024)(128)(4,1)S(1)}, u32[]{:S(2)}) copy-start(pred[1536]{0:T(1024)(128)(4,1)S(1)} %compare_reduce_fusion.7) | copy-start | bytes 4612
  22.4 124.1 %copy-start.169 = (f32[16]{0:T(128)}, f32[16]{0:T(128)S(1)}, u32[]{:S(2)}) copy-start(f32[16]{0:T(128)S(1)} %reduce_sum.415) | copy-start | bytes 196
  22.5 129.3 %copy-start.138 = (pred[1536]{0:T(1024)(128)(4,1)}, pred[1536]{0:T(1024)(128)(4,1)S(1)}, u32[]{:S(2)}) copy-start(pred[1536]{0:T(1024)(128)(4,1)S(1)} %compare_reduce_fusion.8) | copy-start | bytes 4612
  27.8 138.2 %copy-start.53 = (f32[1,2,8,128]{3,1,2,0:T(2,128)}, f32[1,2,8,128]{3,1,2,0:T(2,128)S(1)}, u32[]{:S(2)}) copy-start(f32[1,2,8,128]{3,1,2,0:T(2,128)S(1)} %copy.360) | copy-start | bytes 24580
  28.8 137.2 %copy-start.213 = (f32[2048]{0:T(1024)}, f32[2048]{0:T(1024)S(1)}, u32[]{:S(2)}) copy-start(f32[2048]{0:T(1024)S(1)} %broadcast_multiply_fusion.15) | copy-start | bytes 24580
  29.8 136.6 %copy-start.219 = (f32[2048]{0:T(1024)}, f32[2048]{0:T(1024)S(1)}, u32[]{:S(2)}) copy-start(f32[2048]{0:T(1024)S(1)} %get-tuple-element.25) | copy-start | bytes 24580
  29.9 136.2 %copy-start.60 = (f32[15,19]{1,0:T(8,128)S(1)}, f32[15,19]{1,0:T(8,128)}, u32[]{:S(2)}) copy-start(f32[15,19]{1,0:T(8,128)} %constant.153.clone) | copy-start | bytes 3424
  29.9 136.6 %copy-start.35 = (f32[19,6]{1,0:T(8,128)S(1)}, f32[19,6]{1,0:T(8,128)}, u32[]{:S(2)}) copy-start(f32[19,6]{1,0:T(8,128)} %constant.154.clone) | copy-start | bytes 1372
  29.9 136.9 %copy-start.41 = (f32[19,9]{1,0:T(8,128)S(1)}, f32[19,9]{1,0:T(8,128)}, u32[]{:S(2)}) copy-start(f32[19,9]{1,0:T(8,128)} %constant.155.clone) | copy-start | bytes 2056
  29.9 136.9 %copy-start.264 = (f32[19]{0:T(128)S(1)}, f32[19]{0:T(128)}, u32[]{:S(2)}) copy-start(f32[19]{0:T(128)} %constant.157.clone) | copy-start | bytes 232
  38.3 128.1 %copy-start.146 = (f32[1536]{0:T(1024)}, f32[1536]{0:T(1024)S(1)}, u32[]{:S(2)}) copy-start(f32[1536]{0:T(1024)S(1)} %gather_fusion.1) | copy-start | bytes 18436
  49.7 117.0 %copy-start.67 = (pred[1536]{0:T(1024)(128)(4,1)}, pred[1536]{0:T(1024)(128)(4,1)S(1)}, u32[]{:S(2)}) copy-start(pred[1536]{0:T(1024)(128)(4,1)S(1)} %get-tuple-element.39) | copy-start | bytes 4612
  167.6 2.3 collective-permute-start.4
  167.6 4.9 collective-permute-start.5
  172.7 5.6 collective-permute-start.6
  172.8 5.6 collective-permute-start.7
  184.8 126.5 %copy-start.15 = (f32[15,2048]{1,0:T(8,128)}, f32[15,2048]{1,0:T(8,128)S(1)}, u32[]{:S(2)}) copy-start(f32[15,2048]{1,0:T(8,128)S(1)} %fusion.261) | copy-start | bytes 368644
  185.5 125.4 %copy-start.221 = (f32[2048]{0:T(1024)}, f32[2048]{0:T(1024)S(1)}, u32[]{:S(2)}) copy-start(f32[2048]{0:T(1024)S(1)} %get-tuple-element.29) | copy-start | bytes 24580
  185.6 125.3 %copy-start.36 = (f32[19,6]{1,0:T(8,128)S(1)}, f32[19,6]{1,0:T(8,128)}, u32[]{:S(2)}) copy-start(f32[19,6]{1,0:T(8,128)} %constant.154.clone) | copy-start | bytes 1372
  185.6 125.7 %copy-start.42 = (f32[19,9]{1,0:T(8,128)S(1)}, f32[19,9]{1,0:T(8,128)}, u32[]{:S(2)}) copy-start(f32[19,9]{1,0:T(8,128)} %constant.155.clone) | copy-start | bytes 2056
  185.6 125.7 %copy-start.265 = (f32[19]{0:T(128)S(1)}, f32[19]{0:T(128)}, u32[]{:S(2)}) copy-start(f32[19]{0:T(128)} %constant.157.clone) | copy-start | bytes 232
  194.1 117.2 %copy-start.149 = (f32[1536]{0:T(1024)}, f32[1536]{0:T(1024)S(1)}, u32[]{:S(2)}) copy-start(f32[1536]{0:T(1024)S(1)} %gather_fusion.3) | copy-start | bytes 18436
  312.1 2.9 collective-permute-start.8
  313.2 4.7 collective-permute-start.9
  318.0 6.5 collective-permute-start.10
  318.1 6.5 collective-permute-start.11
  331.0 126.3 %copy-start.17 = (f32[15,2048]{1,0:T(8,128)}, f32[15,2048]{1,0:T(8,128)S(1)}, u32[]{:S(2)}) copy-start(f32[15,2048]{1,0:T(8,128)S(1)} %fusion.257) | copy-start | bytes 368644
  331.7 125.2 %copy-start.223 = (f32[2048]{0:T(1024)}, f32[2048]{0:T(1024)S(1)}, u32[]{:S(2)}) copy-start(f32[2048]{0:T(1024)S(1)} %get-tuple-element.33) | copy-start | bytes 24580
  331.8 125.1 %copy-start.37 = (f32[19,6]{1,0:T(8,128)S(1)}, f32[19,6]{1,0:T(8,128)}, u32[]{:S(2)}) copy-start(f32[19,6]{1,0:T(8,128)} %constant.154.clone) | copy-start | bytes 1372
  331.8 125.5 %copy-start.43 = (f32[19,9]{1,0:T(8,128)S(1)}, f32[19,9]{1,0:T(8,128)}, u32[]{:S(2)}) copy-start(f32[19,9]{1,0:T(8,128)} %constant.155.clone) | copy-start | bytes 2056
  331.8 125.5 %copy-start.267 = (f32[19]{0:T(128)S(1)}, f32[19]{0:T(128)}, u32[]{:S(2)}) copy-start(f32[19]{0:T(128)} %constant.157.clone) | copy-start | bytes 232
  458.1 14.2 %collective-permute-start.12 = (f32[19,1,16,16]{3,2,1,0:T(8,128)S(1)}, f32[19,1,16,16]{3,2,1,0:T(8,128)S(1)}, u32[]{:S(2)}, u32[]{:S(2)}) collective-permute-start(f32[19,1,16,16]{3,2,1,0:T(8,128)S(1)} %get-tuple-element.65), channel_id=1, source_target_pairs={{0,8},{8,16},{16,24},{24,32},{32,40},{40,48},{48,56},{56,64},{64,7... | collective-permute-start | bytes 58376 | tf_op jit(solution)/shard_map/ppermute | solution.py:25
  470.7 4.7 collective-permute-start.13
  476.6 10.6 collective-permute-start.14
  476.7 10.5 collective-permute-start.15
  501.9 124.2 %copy-start.233 = (f32[1536]{0:T(1024)}, f32[1536]{0:T(1024)S(1)}, u32[]{:S(2)}) copy-start(f32[1536]{0:T(1024)S(1)} %gather_fusion.8) | copy-start | bytes 18436
  627.1 4.3 collective-permute-start.16
  627.2 4.7 collective-permute-start.17
  632.1 8.7 collective-permute-start.18
  633.7 7.1 collective-permute-start.19
  779.6 3.4 collective-permute-start.20
  779.7 4.7 collective-permute-start.21
  784.6 8.8 collective-permute-start.22
  784.7 8.7 collective-permute-start.23
  931.0 3.3 collective-permute-start.24
  931.1 4.7 collective-permute-start.25
  936.0 8.9 collective-permute-start.26
  936.1 8.8 collective-permute-start.27
  1082.5 7.0 collective-permute-start.28
  1082.6 7.0 collective-permute-start.29
  1089.8 135.3 %collective-permute-start.30 = (f32[19,10,1,16]{3,2,1,0:T(1,128)S(1)}, f32[19,10,1,16]{3,2,1,0:T(1,128)S(1)}, u32[]{:S(2)}, u32[]{:S(2)}) collective-permute-start(f32[19,10,1,16]{3,2,1,0:T(1,128)S(1)} %get-tuple-element.40), channel_id=1, source_target_pairs={{0,1},{1,2},{2,3},{3,4},{4,5},{5,6},{6,7},{7,0},{8,9},{9,10},{10,1... | collective-permute-start | bytes 36488 | tf_op jit(solution)/shard_map/ppermute | solution.py:25
  1090.8 134.2 %collective-permute-start.31 = (f32[19,10,1,16]{3,2,1,0:T(1,128)S(1)}, f32[19,10,1,16]{3,2,1,0:T(1,128)S(1)}, u32[]{:S(2)}, u32[]{:S(2)}) collective-permute-start(f32[19,10,1,16]{3,2,1,0:T(1,128)S(1)} %get-tuple-element.41), channel_id=1, source_target_pairs={{1,0},{2,1},{3,2},{4,3},{5,4},{6,5},{7,6},{0,7},{9,8},{10,9},{11,1... | collective-permute-start | bytes 36488 | tf_op jit(solution)/shard_map/ppermute | solution.py:26
  (244 other events, 8801.4 us)
